TPU v7x, 128 devices: a whole 4x4x4 slice. The times are simulated.
128 devices in a mesh: row: 8 (over x, z_lo), col: 16 (over z_hi, y, core).
Axes of the slice: x: 4, y: 4, z: 4 (z_hi: 2, z_lo: 2; z = z_hi * 2 + z_lo), core: 2. Of those that a mesh axis runs over, the one named last changes fastest.
Arguments:
- a_cols: bfloat16 [16384, 8192], P('row', 'col'), may hold values from -6 to 6
- owners: int32 [1024], replicated, may hold values from 0 to 15
- column_slot: int32 [1024], replicated, may hold values from 0 to 511
- update_flag: int32 [1024], replicated, may hold values from 0 to 1
- rescale: float32 [1024], replicated, may hold values from 0.5 to 2
- inverses: bfloat16 [2, 512, 512], replicated, may hold values from -0.0078125 to 0.0078125
- trailing: float32 [16384, 16384], P('row', 'col'), may hold values from -0.15625 to 0.15625
Outputs:
- updated_slab: float32 [16384, 16384], P('row', 'col')
- panels: bfloat16 [16384, 1024], P('row')
All inputs are finite; a program needn't handle non-finite values.
Results may differ from a plain program's by a relative error of at most 0.013.
The roundings to bfloat16 on the way count: a program that leaves them out, or rounds other values in their place, can miss the bound.
Values may be sent and summed in bfloat16 or wider, within the bound.
No kernel may reach another device: no remote copies, remote signals or barrier semaphores. Data moves between devices by JAX's collectives and lax.ppermute only.
A program may use at most 128 MiB of HBM per device.

v0:
```python
import jax
import jax.numpy as jnp
from jax import lax
from jax.sharding import PartitionSpec as P


def from_root(value, axis, source):
    kept = jnp.where(lax.axis_index(axis) == source, value, 0).astype(value.dtype)
    return lax.psum(kept, axis)


def panel_pass(columns, inverses, signed, reducer):
    width = inverses.shape[1]
    first_cols = columns[:, :width]
    second_cols = columns[:, width:]
    first_panel = jnp.dot(first_cols, inverses[0], preferred_element_type=jnp.float32).astype(
        jnp.bfloat16
    )
    gram_block = reducer(
        lax.dot_general(
            first_panel, second_cols, (((0,), (0,)), ((), ())), preferred_element_type=jnp.float32
        )
    )
    weighted = first_panel * signed[:width][None, :]
    coupled = (
        second_cols.astype(jnp.float32)
        - jnp.dot(weighted, gram_block.astype(jnp.bfloat16), preferred_element_type=jnp.float32)
    ).astype(jnp.bfloat16)
    second_panel = jnp.dot(coupled, inverses[1], preferred_element_type=jnp.float32).astype(
        jnp.bfloat16
    )
    return jnp.concatenate([first_panel, second_panel], axis=1)


def body(a_cols, owners, column_slot, update_flag, rescale, inverses, trailing):
    column_index = lax.axis_index("col")
    picked = jnp.take(a_cols, column_slot, axis=1)
    owned = owners == column_index
    partial_cols = jnp.where(owned[None, :], picked, jnp.zeros((), jnp.bfloat16))
    signed = (2 * update_flag - 1).astype(jnp.bfloat16)
    summed = lax.psum(partial_cols, "col").astype(jnp.float32)
    columns = (summed * rescale[None, :]).astype(jnp.bfloat16)
    panels = panel_pass(columns, inverses, signed, lambda matrix: lax.psum(matrix, "row"))
    block_rows = panels.shape[0]
    block_cols = trailing.shape[1]
    source = column_index * block_cols // block_rows
    offset = column_index * block_cols % block_rows
    strip_rows = lax.dynamic_slice_in_dim(panels, offset, block_cols, 0)
    column_panels = from_root(strip_rows, "row", source)
    weighted = panels * signed[None, :]
    update = lax.dot_general(
        weighted, column_panels, (((1,), (1,)), ((), ())), preferred_element_type=jnp.float32
    )
    return (trailing + update, panels)


def solution(mesh):
    placed = (P("row", "col"), P(), P(), P(), P(), P(), P("row", "col"))
    return jax.shard_map(
        body,
        mesh=mesh,
        in_specs=placed,
        out_specs=(P("row", "col"), P("row", None)),
        check_vma=False,
    )
```

profile of v0, /device:TPU:8, one launch (start us, length us, event | category | flops | bytes accessed | tf_op | source)
XLA Modules:
  0.0 379.0 jit_solution(7499403749165712552)
XLA Ops:
  7.2 0.0 copy-start.1
  7.2 0.0 copy-start.6
  7.2 0.0 all-reduce.4.cloned.1.call-start
  7.2 2.9 copy.9
  10.2 0.0 copy-done.6
  10.2 6.0 %gather_fusion = bf16[1024,2048]{1,0:T(8,128)(2,1)} fusion(bf16[2048,512]{0,1:T(8,128)(2,1)S(1)} %copy.9, s32[1024]{0:T(1024)S(1)} %fusion.22), kind=kCustom, calls=%fused_computation | custom fusion | bytes 8392704 | tf_op jit(solution)/shard_map/jit(_take)/gather | solution.py:37
  16.2 4.1 %select_bitcast_fusion = bf16[2048,1024]{0,1:T(8,128)(2,1)} fusion(bf16[1024,2048]{1,0:T(8,128)(2,1)} %gather_fusion, pred[1024]{0:T(1024)(128)(4,1)S(1)} %get-tuple-element.5, pred[1024]{0:T(1024)(128)(4,1)S(1)} %get-tuple-element.4), kind=kLoop, calls=%fused_computation.5 | loop fusion | flops 4194304 | bytes 8390656 | tf_op jit(solution)/shard_map/jit(_where)/select_n | solution.py:39
  20.3 0.0 all-reduce.4.cloned.1.call-update
  20.3 0.0 all-reduce.6.cloned.1.call-start
  20.4 0.6 copy-done.5
  21.0 147.4 %all-reduce.4.cloned.1.call-done = bf16[2048,1024]{0,1:T(8,128)(2,1)} async-done(((bf16[2048,1024]{0,1:T(8,128)(2,1)}), bf16[2048,1024]{0,1:T(8,128)(2,1)}) %all-reduce.4.cloned.1.call-update) | async-done | bytes 4194320 | tf_op jit(solution)/shard_map/psum | solution.py:41
  168.4 2.9 multiply_convert_fusion
  171.3 0.0 copy-start
  171.3 1.3 convolution_convert_fusion.1
  172.7 0.7 copy-done
  173.3 1.3 fusion.10
  174.6 69.1 %all-reduce.7 = bf16[512,512]{1,0:T(8,128)(2,1)} all-reduce(f32[512,512]{1,0:T(8,128)S(1)} %fusion.10), channel_id=1, replica_groups=mesh['row'=8,'col'=16] {'row'}, use_global_device_ids=true, to_apply=%region_1.2 | all-reduce | flops 262144 | bytes 1572864 | tf_op jit(solution)/shard_map/psum | solution.py:43
  243.7 5.7 %convolution_convert_fusion = bf16[2048,512]{0,1:T(8,128)(2,1)} fusion(bf16[2048,512]{0,1:T(8,128)(2,1)S(1)} %convolution_convert_fusion.1, bf16[2048,1024]{0,1:T(8,128)(2,1)} %copy-done, bf16[512]{0:T(512)(128)(2,1)S(1)} %slice-done, bf16[2,512,512]{2,1,0:T(8,128)(2,1)} %param.12, bf16[512,512]{1,0:T(8,128)(2,1)} %all-reduce.7), kind=kOutput, calls=%fused_computation.10 | convolution fusion | flops 2152726528 | bytes 7341056 | tf_op jit(solution)/shard_map/dot_general | solution.py:29
  249.4 3.1 fusion.6
  252.5 0.0 all-reduce.6.cloned.1.call-update
  252.5 4.2 %pad_maximum_fusion = bf16[2048,1024]{0,1:T(8,128)(2,1)} fusion(bf16[2048,512]{0,1:T(8,128)(2,1)} %convolution_convert_fusion, bf16[2048,512]{0,1:T(8,128)(2,1)S(1)} %convolution_convert_fusion.1), kind=kLoop, calls=%fused_computation.3 | loop fusion | flops 8388608 | bytes 8388608 | tf_op jit(solution)/shard_map/concatenate | solution.py:32
  256.7 6.4 %copy.10 = bf16[2048,1024]{1,0:T(8,128)(2,1)} copy(bf16[2048,1024]{0,1:T(8,128)(2,1)} %pad_maximum_fusion) | data formatting | bytes 8388608
  263.1 96.3 %all-reduce.6.cloned.1.call-done = bf16[1024,1024]{0,1:T(8,128)(2,1)} async-done(((bf16[1024,1024]{0,1:T(8,128)(2,1)}), bf16[1024,1024]{0,1:T(8,128)(2,1)}) %all-reduce.6.cloned.1.call-update) | async-done | bytes 2097168 | tf_op jit(solution)/shard_map/psum | solution.py:9
  359.4 12.8 %fusion.2 = f32[2048,1024]{1,0:T(8,128)} fusion(f32[2048,1024]{1,0:T(8,128)} %param.13, bf16[1024,1024]{0,1:T(8,128)(2,1)} %all-reduce.6.cloned.1.call-done, bf16[1024]{0:T(1024)(128)(2,1)S(1)} %copy-done.3, bf16[2048,512]{0,1:T(8,128)(2,1)} %convolution_convert_fusion, bf16[2048,512]{0,1:T(8,128)(2,1)S(1)} %convolution_convert_fusion.1), kind=kOutput, calls=%fused_computation.9 | convolution fusion | flops 4309647360 | bytes 23070720 | tf_op jit(solution)/shard_map/dot_general | solution.py:51
  (15 shorter events, 0.0 us)
Async XLA Ops:
  7.2 3.0 copy-start.1
  7.2 3.0 copy-start.6
  7.2 161.2 %all-reduce.4.cloned.1.call-start = ((), (), s32[]{:S(2)}) async-start(), calls=%async_computation | async-start | bytes 8388608 | tf_op jit(solution)/shard_map/psum | solution.py:41
  20.3 0.7 copy-start.5
  20.3 148.1 %copy-start.4 = (f32[1024]{0:T(1024)S(1)}, f32[1024]{0:T(1024)}, u32[]{:S(2)}) copy-start(f32[1024]{0:T(1024)} %param.11) | copy-start | bytes 12292
  20.3 339.1 %all-reduce.6.cloned.1.call-start = ((), (), s32[]{:S(2)}) async-start(), calls=%async_computation.1 | async-start | bytes 4194304 | tf_op jit(solution)/shard_map/psum | solution.py:9
  21.0 150.3 %copy-start.2 = (bf16[1024]{0:T(1024)(128)(2,1)}, bf16[1024]{0:T(1024)(128)(2,1)S(1)}, u32[]{:S(2)}) copy-start(bf16[1024]{0:T(1024)(128)(2,1)S(1)} %add_convert_fusion) | copy-start | bytes 6148
  21.0 150.3 %copy-start.7 = (bf16[2,512,512]{2,1,0:T(8,128)(2,1)S(1)}, bf16[2,512,512]{2,1,0:T(8,128)(2,1)}, u32[]{:S(2)}) copy-start(bf16[2,512,512]{2,1,0:T(8,128)(2,1)} %param.12) | copy-start | bytes 3145732
  171.3 2.0 copy-start
  173.3 70.4 %slice-start = ((bf16[1024]{0:T(1024)(128)(2,1)}), bf16[512]{0:T(512)(128)(2,1)S(1)}, s32[]{:S(2)}) async-start(bf16[1024]{0:T(1024)(128)(2,1)} %copy-done.2), calls=%async_computation.2 | async-start | bytes 2048 | tf_op jit(solution)/shard_map/slice | solution.py:24
  256.7 102.7 %copy-start.3 = (bf16[1024]{0:T(1024)(128)(2,1)S(1)}, bf16[1024]{0:T(1024)(128)(2,1)}, u32[]{:S(2)}) copy-start(bf16[1024]{0:T(1024)(128)(2,1)} %copy-done.2) | copy-start | bytes 6148
Sparse Core Ops, SparseCore 0:
  20.4 147.8 all-reduce.3
  252.6 106.7 all-reduce.5
where the time goes:
time: 380 us; the launch traced here: 379 us
  waiting for transfers between devices  244 us (64%)
  blocking collectives  69.1 us (18%)
  matrix products  21.1 us (6%)
  local copies, waits for them, and re-layouts  16.6 us (4%)
  other arithmetic  14.3 us (4%)
  between operations  14.2 us (4%)
    psum x1, waiting for transfers between devices, body(): summed = lax.psum(partial_cols, 'col').astype(jnp.float32)  147 us
    psum x1, waiting for transfers between devices, from_root(): return lax.psum(kept, axis)  96.3 us
    psum x1, blocking collectives, body(): lax.psum(matrix, 'row')  69.1 us
    dot_general x1, matrix products, body(): lax.dot_general(weighted, column_panels, (((1,), (1,)), ((), ())), prefer...  12.8 us
    unnamed x18, local copies, waits for them, and re-layouts  10.6 us
  transfers between devices with their start and end apart: 2, of which 2 were waited for; matrix products, arithmetic and copies ran while one was open for 3% of the time, Pallas kernels for 0%

commit v1 on v0

--- a/solution.py
+++ b/solution.py
@@ -40,7 +40,9 @@
     signed = (2 * update_flag - 1).astype(jnp.bfloat16)
     summed = lax.psum(partial_cols, "col").astype(jnp.float32)
     columns = (summed * rescale[None, :]).astype(jnp.bfloat16)
-    panels = panel_pass(columns, inverses, signed, lambda matrix: lax.psum(matrix, "row"))
+    panels = panel_pass(
+        columns, inverses, signed, lambda matrix: jnp.sum(lax.all_gather(matrix, "row"), axis=0)
+    )
     block_rows = panels.shape[0]
     block_cols = trailing.shape[1]
     source = column_index * block_cols // block_rows

time: 380 us -> 491 us (1.29)
  waiting for transfers between devices: 244 us -> 419 us
  blocking collectives: 69.1 us -> 0 us
    all_gather x0 -> x1, waiting for transfers between devices: none -> 174 us  [body(): lax.all_gather(matrix, 'row')]
    psum x1 -> x0, blocking collectives: 69.1 us -> none  [body(): lax.psum(matrix, 'row')]
    unnamed x18 -> x14, local copies, waits for them, and re-layouts: 10.6 us -> 10 us
  transfers between devices with their start and end apart: 2 -> 3, of which waited for: 2 -> 3; matrix products, arithmetic and copies ran while one was open for 3% -> 2% of each run, Pallas kernels for 0% -> 0%
where the time goes in v1:
time: 491 us; the launch traced here: 490 us
  waiting for transfers between devices  419 us (85%)
  matrix products  21.9 us (4%)
  other arithmetic  18.8 us (4%)
  local copies, waits for them, and re-layouts  16 us (3%)
  between operations  13.9 us (3%)
    all_gather x1, waiting for transfers between devices, body(): lax.all_gather(matrix, 'row')  174 us
    psum x1, waiting for transfers between devices, body(): summed = lax.psum(partial_cols, 'col').astype(jnp.float32)  148 us
    psum x1, waiting for transfers between devices, from_root(): return lax.psum(kept, axis)  97.1 us
    dot_general x1, matrix products, body(): lax.dot_general(weighted, column_panels, (((1,), (1,)), ((), ())), prefer...  12.8 us
    unnamed x14, local copies, waits for them, and re-layouts  10 us
  transfers between devices with their start and end apart: 3, of which 3 were waited for; matrix products, arithmetic and copies ran while one was open for 2% of the time, Pallas kernels for 0%

profile of v1, /device:TPU:8, one launch (start us, length us, event | category | flops | bytes accessed | tf_op | source)
XLA Modules:
  0.0 490.1 jit_solution(4044500137306189386)
XLA Ops:
  7.2 0.0 all-reduce.3.cloned.1.call-start
  7.2 2.9 copy.9
  10.2 6.0 %gather_fusion = bf16[1024,2048]{1,0:T(8,128)(2,1)} fusion(bf16[2048,512]{0,1:T(8,128)(2,1)S(1)} %copy.9, s32[1024]{0:T(1024)S(1)} %fusion.22), kind=kCustom, calls=%fused_computation | custom fusion | bytes 8392704 | tf_op jit(solution)/shard_map/jit(_take)/gather | solution.py:37
  16.2 4.1 select_bitcast_fusion
  20.3 0.0 all-reduce.3.cloned.1.call-update
  20.3 0.0 copy-start.5
  20.3 0.0 all-gather.3.cloned.1.call-start
  20.4 148.0 %all-reduce.3.cloned.1.call-done = bf16[2048,1024]{0,1:T(8,128)(2,1)} async-done(((bf16[2048,1024]{0,1:T(8,128)(2,1)}), bf16[2048,1024]{0,1:T(8,128)(2,1)}) %all-reduce.3.cloned.1.call-update) | async-done | bytes 4194320 | tf_op jit(solution)/shard_map/psum | solution.py:41
  168.4 2.9 multiply_convert_fusion
  171.3 0.0 copy-start
  171.3 1.3 convolution_convert_fusion.1
  172.6 0.7 copy-done
  173.3 2.3 fusion.10
  175.6 0.0 all-gather.3.cloned.1.call-update
  175.6 0.2 all-reduce.5.cloned.1.call-start
  175.9 174.1 %all-gather.3.cloned.1.call-done = f32[4096,512]{1,0:T(8,128)} async-done(((f32[512,512]{1,0:T(8,128)}), f32[4096,512]{1,0:T(8,128)}) %all-gather.3.cloned.1.call-update) | async-done | bytes 8388624 | tf_op jit(solution)/shard_map/all_gather | solution.py:44
  350.0 4.4 reduce_sum.9
  354.4 5.6 %convolution_convert_fusion = bf16[2048,512]{0,1:T(8,128)(2,1)} fusion(bf16[2048,512]{0,1:T(8,128)(2,1)S(1)} %convolution_convert_fusion.1, bf16[2048,1024]{0,1:T(8,128)(2,1)} %copy-done, bf16[512]{0:T(512)(128)(2,1)S(1)} %slice.18, bf16[2,512,512]{2,1,0:T(8,128)(2,1)} %param.12, bf16[512,512]{1,0:T(8,128)(2,1)S(1)} %reduce_sum.9), kind=kOutput, calls=%fused_computation.10 | convolution fusion | flops 2152726528 | bytes 7341056 | tf_op jit(solution)/shard_map/dot_general | solution.py:29
  360.0 3.1 fusion.6
  363.1 0.0 all-reduce.5.cloned.1.call-update
  363.1 4.2 pad_maximum_fusion
  367.3 6.4 %copy.10 = bf16[2048,1024]{1,0:T(8,128)(2,1)} copy(bf16[2048,1024]{0,1:T(8,128)(2,1)} %pad_maximum_fusion) | data formatting | bytes 8388608
  373.7 97.1 %all-reduce.5.cloned.1.call-done = bf16[1024,1024]{0,1:T(8,128)(2,1)} async-done(((bf16[1024,1024]{0,1:T(8,128)(2,1)}), bf16[1024,1024]{0,1:T(8,128)(2,1)}) %all-reduce.5.cloned.1.call-update) | async-done | bytes 2097168 | tf_op jit(solution)/shard_map/psum | solution.py:9
  470.8 12.8 %fusion.2 = f32[2048,1024]{1,0:T(8,128)} fusion(f32[2048,1024]{1,0:T(8,128)} %param.13, bf16[1024,1024]{0,1:T(8,128)(2,1)} %all-reduce.5.cloned.1.call-done, bf16[1024]{0:T(1024)(128)(2,1)S(1)} %add_convert_fusion, bf16[2048,512]{0,1:T(8,128)(2,1)} %convolution_convert_fusion, bf16[2048,512]{0,1:T(8,128)(2,1)S(1)} %convolution_convert_fusion.1), kind=kOutput, calls=%fused_computation.9 | convolution fusion | flops 4309647360 | bytes 23070720 | tf_op jit(solution)/shard_map/dot_general | solution.py:53
  (13 shorter events, 0.0 us)
Async XLA Ops:
  7.2 3.0 copy-start.1
  7.2 3.0 copy-start.4
  7.2 161.2 %all-reduce.3.cloned.1.call-start = ((), (), s32[]{:S(2)}) async-start(), calls=%async_computation | async-start | bytes 8388608 | tf_op jit(solution)/shard_map/psum | solution.py:41
  20.3 148.1 %copy-start.2 = (f32[1024]{0:T(1024)S(1)}, f32[1024]{0:T(1024)}, u32[]{:S(2)}) copy-start(f32[1024]{0:T(1024)} %param.11) | copy-start | bytes 12292
  20.3 151.0 %copy-start.5 = (bf16[2,512,512]{2,1,0:T(8,128)(2,1)S(1)}, bf16[2,512,512]{2,1,0:T(8,128)(2,1)}, u32[]{:S(2)}) copy-start(bf16[2,512,512]{2,1,0:T(8,128)(2,1)} %param.12) | copy-start | bytes 3145732
  20.3 329.7 %all-gather.3.cloned.1.call-start = ((), (), s32[]{:S(2)}) async-start(), calls=%async_computation.2 | async-start | bytes 9437184 | tf_op jit(solution)/shard_map/all_gather | solution.py:44
  171.3 2.0 copy-start
  173.3 2.5 copy-start.3
  175.6 295.2 %all-reduce.5.cloned.1.call-start = ((), (), s32[]{:S(2)}) async-start(), calls=%async_computation.1 | async-start | bytes 4194304 | tf_op jit(solution)/shard_map/psum | solution.py:9
Sparse Core Ops, SparseCore 0:
  20.4 147.8 all-reduce.2
  175.7 174.2 all-gather.2
  363.2 107.4 all-reduce.4
